TPU v7x, 32 devices: a whole 2x2x4 slice. The times are simulated.
32 devices in a mesh: gx: 8 (over y, x, core), gy: 4 (over z).
Axes of the slice: x: 2, y: 2, z: 4, core: 2. Of those that a mesh axis runs over, the one named last changes fastest.
Arguments:
- activations: bfloat16 [1024, 7168], P('gx', 'gy'), may hold values from -6 to 6
- out_grad: bfloat16 [1024, 7168], P('gx', 'gy'), may hold values from -0.59765625 to 0.59765625
- saved_gate: bfloat16 [1024, 2, 1024], P('gx', None, 'gy'), may hold values from -9 to 9
- saved_up: bfloat16 [1024, 2, 1024], P('gx', None, 'gy'), may hold values from -6 to 6
- route_ids: int32 [1024, 2], P('gx'), may hold values from 0 to 7, all different within a row; in each aligned block of 128 rows (0 to 127, 128 to 255, ...) at most 48 rows name the same one
- route_weight: float32 [1024, 2], P('gx'), may hold values from 0.1 to 1
- down_weight: bfloat16 [8, 1024, 7168], P('gx', None, 'gy'), may hold values from -0.1875 to 0.1875
Outputs:
- grad_gate: bfloat16 [8, 7168, 1024], P('gx', 'gy')
- grad_up: bfloat16 [8, 7168, 1024], P('gx', 'gy')
- grad_down: bfloat16 [8, 1024, 7168], P('gx', None, 'gy')
Inputs may be any that keep to these rules, and one draw needn't show every extreme that they name: `route_ids`: each token names 2 different experts. Within each aligned block of 128 tokens (one index of gx) no expert is named by more than 48 tokens, a bound that some block reaches.
All inputs are finite; a program needn't handle non-finite values.
Results may differ from a plain program's by a relative error of at most 0.02.
Values may be sent and summed in bfloat16 or wider, within the bound.
A program may use at most 64 MiB of HBM per device.

v0:
```python
import jax
import jax.numpy as jnp
from jax import lax
from jax.sharding import PartitionSpec as P

MOST = 48


def local_grads(hidden_grad, gate_rows, up_rows):
    gate_val = gate_rows.astype(jnp.float32)
    up_val = up_rows.astype(jnp.float32)
    gate_sig = jax.nn.sigmoid(gate_val)
    silu_val = gate_val * gate_sig
    hidden_act = (silu_val * up_val).astype(jnp.bfloat16)
    grad_upper = (hidden_grad * silu_val).astype(jnp.bfloat16)
    grad_gated = (hidden_grad * up_val * gate_sig * (1.0 + gate_val * (1.0 - gate_sig))).astype(
        jnp.bfloat16
    )
    return (hidden_act, grad_gated, grad_upper)


def contract_rows(left, right):
    return lax.dot_general(
        left, right, (((0,), (0,)), ((), ())), preferred_element_type=jnp.float32
    ).astype(jnp.bfloat16)


def slot_rows(route_ids, experts):
    flat_ids = route_ids.reshape(-1)
    onehot = (flat_ids[:, None] == jnp.arange(experts, dtype=jnp.int32)[None, :]).astype(jnp.int32)
    rank_in = jnp.sum((jnp.cumsum(onehot, axis=0) - onehot) * onehot, axis=1)
    return flat_ids * MOST + rank_in


def pack_rows(values, target, experts):
    buffer = jnp.zeros((experts * MOST, values.shape[-1]), values.dtype).at[target].set(values)
    return buffer.reshape(experts, MOST, values.shape[-1])


def merge_rows(values):
    return values.reshape(-1, values.shape[-1])


def on_device(activations, out_grad, saved_gate, saved_up, route_ids, route_weight, down_weight):
    experts = lax.axis_size("gx")
    top_count = route_ids.shape[1]
    target = slot_rows(route_ids, experts)
    act_routes = pack_rows(jnp.repeat(activations, top_count, axis=0), target, experts)
    scaled = (
        route_weight.reshape(-1, 1) * jnp.repeat(out_grad, top_count, axis=0).astype(jnp.float32)
    ).astype(jnp.bfloat16)
    grad_routes = pack_rows(scaled, target, experts)
    gate_routes = pack_rows(saved_gate.reshape(-1, saved_gate.shape[-1]), target, experts)
    up_routes = pack_rows(saved_up.reshape(-1, saved_up.shape[-1]), target, experts)
    rows_act, rows_grad, gate_rows, up_rows = (
        lax.all_to_all(act_routes, "gx", split_axis=0, concat_axis=0, tiled=True),
        lax.all_to_all(grad_routes, "gx", split_axis=0, concat_axis=0, tiled=True),
        lax.all_to_all(gate_routes, "gx", split_axis=0, concat_axis=0, tiled=True),
        lax.all_to_all(up_routes, "gx", split_axis=0, concat_axis=0, tiled=True),
    )
    rows_grad = merge_rows(rows_grad)
    gate_rows = merge_rows(gate_rows)
    up_rows = merge_rows(up_rows)
    weight = down_weight[0]
    partial_value = lax.dot_general(
        rows_grad, weight, (((1,), (1,)), ((), ())), preferred_element_type=jnp.float32
    )
    rows_act = merge_rows(rows_act)
    hidden_grad = lax.psum(partial_value.astype(jnp.bfloat16), "gy").astype(jnp.float32)
    gate_full, up_full = (
        lax.all_gather(gate_rows, "gy", axis=1, tiled=True),
        lax.all_gather(up_rows, "gy", axis=1, tiled=True),
    )
    hidden_act, grad_gated, grad_upper = local_grads(hidden_grad, gate_full, up_full)
    grad_gate = contract_rows(rows_act, grad_gated)[None]
    grad_up = contract_rows(rows_act, grad_upper)[None]
    grad_down = contract_rows(hidden_act, rows_grad)[None]
    return (grad_gate, grad_up, grad_down)


def solution(mesh):
    placed = (
        P("gx", "gy"),
        P("gx", "gy"),
        P("gx", None, "gy"),
        P("gx", None, "gy"),
        P("gx", None),
        P("gx", None),
        P("gx", None, "gy"),
    )
    return jax.shard_map(
        on_device,
        mesh=mesh,
        in_specs=placed,
        out_specs=(P("gx", "gy", None), P("gx", "gy", None), P("gx", None, "gy")),
        check_vma=False,
    )
```

profile of v0, /device:TPU:0, one launch (start us, length us, event | category | flops | bytes accessed | tf_op | source)
XLA Modules:
  0.0 144.9 jit_solution(7677745777979854261)
XLA Ops:
  7.2 0.7 broadcast_multiply_fusion
  7.9 0.8 copy.11
  9.3 0.6 reduce-window.6
  10.1 1.0 reshape.129
  11.2 2.1 %scatter_custom_fusion.3 = bf16[384,256]{1,0:T(8,128)(2,1)} fusion(s32[256]{0:T(256)S(1)} %bitcast.42, bf16[256,256]{1,0:T(8,128)(2,1)S(1)} %reshape.129, bf16[]{:T(256)} %constant.5.clone.1), kind=kCustom, calls=%fused_computation.35 | custom fusion | bytes 196610 | tf_op jit(solution)/shard_map/scatter | solution.py:36
  13.3 5.2 %all-to-all-start.3 = ((bf16[8,48,256]{2,1,0:T(8,128)(2,1)}), bf16[8,48,256]{2,1,0:T(8,128)(2,1)S(1)}, u32[]{:S(2)}, u32[]{:S(2)}) async-start(bf16[8,48,256]{2,1,0:T(8,128)(2,1)} %bitcast.11), calls=%async_computation.3 | async-start | bytes 393216 | tf_op jit(solution)/shard_map/all_to_all | solution.py:58
  18.5 1.0 reshape.121
  19.4 2.1 %scatter_custom_fusion.2 = bf16[384,256]{1,0:T(8,128)(2,1)} fusion(s32[256]{0:T(256)S(1)} %bitcast.43, bf16[256,256]{1,0:T(8,128)(2,1)S(1)} %reshape.121, bf16[]{:T(256)} %constant.5.clone.1), kind=kCustom, calls=%fused_computation.37 | custom fusion | bytes 196610 | tf_op jit(solution)/shard_map/scatter | solution.py:36
  21.5 3.1 %all-to-all-done.3 = bf16[8,48,256]{2,1,0:T(8,128)(2,1)S(1)} async-done(((bf16[8,48,256]{2,1,0:T(8,128)(2,1)}), bf16[8,48,256]{2,1,0:T(8,128)(2,1)S(1)}, u32[]{:S(2)}, u32[]{:S(2)}) %all-to-all-start.3) | async-done | bytes 196640 | tf_op jit(solution)/shard_map/all_to_all | solution.py:58
  24.7 0.7 copy-done
  25.4 3.4 %all-to-all-start.2 = ((bf16[8,48,256]{2,1,0:T(8,128)(2,1)}), bf16[8,48,256]{2,1,0:T(8,128)(2,1)S(1)}, u32[]{:S(2)}, u32[]{:S(2)}) async-start(bf16[8,48,256]{2,1,0:T(8,128)(2,1)} %bitcast.9), calls=%async_computation.2 | async-start | bytes 393216 | tf_op jit(solution)/shard_map/all_to_all | solution.py:59
  29.0 1.7 %broadcast_in_dim.21 = f32[128,2,1792]{2,1,0:T(2,128)} broadcast(bf16[128,1792]{1,0:T(8,128)(2,1)S(1)} %copy-done.1), dimensions={0,2} | broadcast | bytes 2293760 | tf_op jit(solution)/shard_map/broadcast_in_dim | solution.py:50
  30.7 2.5 %convert_element_type.50 = f32[256,1792]{1,0:T(8,128)S(1)} reshape(f32[128,2,1792]{2,1,0:T(2,128)} %broadcast_in_dim.21) | data formatting | bytes 3670016 | tf_op jit(solution)/shard_map/convert_element_type | solution.py:50
  33.3 3.2 %scatter_custom_fusion.1 = bf16[384,1792]{1,0:T(8,128)(2,1)} fusion(s32[256]{0:T(256)S(1)} %bitcast.44, f32[256,1792]{1,0:T(8,128)S(1)} %convert_element_type.50, f32[256]{0:T(256)S(1)} %mul.54, bf16[]{:T(256)} %constant.5.clone.1), kind=kCustom, calls=%fused_computation.29 | custom fusion | flops 917504 | bytes 3212290 | tf_op jit(solution)/shard_map/scatter | solution.py:36
  36.5 4.3 %all-to-all-start.1 = ((bf16[8,48,1792]{2,1,0:T(8,128)(2,1)}), bf16[8,48,1792]{2,1,0:T(8,128)(2,1)S(1)}, u32[]{:S(2)}, u32[]{:S(2)}) async-start(bf16[8,48,1792]{2,1,0:T(8,128)(2,1)} %bitcast.6), calls=%async_computation.1 | async-start | bytes 2752512 | tf_op jit(solution)/shard_map/all_to_all | solution.py:57
  41.6 3.2 %scatter_custom_fusion = bf16[384,1792]{1,0:T(8,128)(2,1)} fusion(s32[256]{0:T(256)S(1)} %bitcast.45, bf16[256,1792]{1,0:T(8,128)(2,1)S(1)} %reshape.105, bf16[]{:T(256)} %constant.5.clone.1), kind=kCustom, calls=%fused_computation.33 | custom fusion | bytes 1376258 | tf_op jit(solution)/shard_map/scatter | solution.py:36
  44.8 20.0 %all_gather.7 = bf16[384,1024]{1,0:T(8,128)(2,1)S(1)} all-gather(bf16[384,256]{1,0:T(8,128)(2,1)} %bitcast.40), channel_id=1, replica_groups=mesh['gx'=8,'gy'=4] {'gy'}, dimensions={1}, use_global_device_ids=true | all-gather | bytes 983040 | tf_op jit(solution)/shard_map/all_gather | solution.py:71
  64.8 4.3 %all-to-all-start = ((bf16[8,48,1792]{2,1,0:T(8,128)(2,1)}), bf16[8,48,1792]{2,1,0:T(8,128)(2,1)}, u32[]{:S(2)}, u32[]{:S(2)}) async-start(bf16[8,48,1792]{2,1,0:T(8,128)(2,1)} %bitcast.4), calls=%async_computation | async-start | bytes 2752512 | tf_op jit(solution)/shard_map/all_to_all | solution.py:56
  69.2 4.5 %fusion.14 = bf16[384,1024]{1,0:T(8,128)(2,1)} fusion(bf16[384,1792]{1,0:T(8,128)(2,1)S(1)} %bitcast.37, bf16[1,1024,1792]{2,1,0:T(8,128)(2,1)} %param.13), kind=kOutput, calls=%fused_computation.28 | convolution fusion | flops 1409679360 | bytes 5832704 | tf_op jit(solution)/shard_map/dot_general | solution.py:65
  73.7 27.0 %all_gather.6 = bf16[384,1024]{1,0:T(8,128)(2,1)S(1)} all-gather(bf16[384,256]{1,0:T(8,128)(2,1)S(1)} %bitcast.39), channel_id=1, replica_groups=mesh['gx'=8,'gy'=4] {'gy'}, dimensions={1}, use_global_device_ids=true | all-gather | bytes 983040 | tf_op jit(solution)/shard_map/all_gather | solution.py:72
  100.8 4.0 %fusion.4 = bf16[1,1024,1792]{2,1,0:T(8,128)(2,1)} fusion(bf16[384,1792]{1,0:T(8,128)(2,1)S(1)} %bitcast.38, bf16[384,1024]{1,0:T(8,128)(2,1)S(1)} %all_gather.6, bf16[384,1024]{1,0:T(8,128)(2,1)S(1)} %all_gather.7), kind=kOutput, calls=%fused_computation.11 | convolution fusion | flops 1414266880 | bytes 6619136 | tf_op jit(solution)/shard_map/dot_general | solution.py:23
  104.8 22.1 %all-reduce.2.cloned.1.call-done = bf16[384,1024]{1,0:T(8,128)(2,1)} async-done(((bf16[384,1024]{1,0:T(8,128)(2,1)}), bf16[384,1024]{1,0:T(8,128)(2,1)}) %all-reduce.2.cloned.1.call-update) | async-done | bytes 786448 | tf_op jit(solution)/shard_map/psum | solution.py:69
  126.9 5.7 %fusion.2 = bf16[1,1792,1024]{2,1,0:T(8,128)(2,1)} fusion(bf16[384,1792]{1,0:T(8,128)(2,1)} %bitcast.5, bf16[384,1024]{1,0:T(8,128)(2,1)S(1)} %all_gather.6, bf16[384,1024]{1,0:T(8,128)(2,1)} %all-reduce.2.cloned.1.call-done, bf16[384,1024]{1,0:T(8,128)(2,1)S(1)} %all_gather.7), kind=kOutput, calls=%fused_computation.9 | convolution fusion | flops 1416232960 | bytes 7405568 | tf_op jit(solution)/shard_map/dot_general | solution.py:23
  132.6 5.4 %fusion.3 = bf16[1,1792,1024]{2,1,0:T(8,128)(2,1)} fusion(bf16[384,1792]{1,0:T(8,128)(2,1)} %bitcast.5, bf16[384,1024]{1,0:T(8,128)(2,1)S(1)} %copy-done.4, bf16[384,1024]{1,0:T(8,128)(2,1)S(1)} %all_gather.7), kind=kOutput, calls=%fused_computation.10 | convolution fusion | flops 1414266880 | bytes 6619136 | tf_op jit(solution)/shard_map/dot_general | solution.py:23
  (28 shorter events, 2.0 us)
Async XLA Ops:
  7.2 21.6 %copy-start.3 = (f32[128,2]{0,1:T(2,128)S(1)}, f32[128,2]{0,1:T(2,128)}, u32[]{:S(2)}) copy-start(f32[128,2]{0,1:T(2,128)} %param.12) | copy-start | bytes 3076
  7.2 21.8 %copy-start.1 = (bf16[128,1792]{1,0:T(8,128)(2,1)S(1)}, bf16[128,1792]{1,0:T(8,128)(2,1)}, u32[]{:S(2)}) copy-start(bf16[128,1792]{1,0:T(8,128)(2,1)} %param.8) | copy-start | bytes 1376260
  13.3 11.4 %all-to-all-start.3 = ((bf16[8,48,256]{2,1,0:T(8,128)(2,1)}), bf16[8,48,256]{2,1,0:T(8,128)(2,1)S(1)}, u32[]{:S(2)}, u32[]{:S(2)}) async-start(bf16[8,48,256]{2,1,0:T(8,128)(2,1)} %bitcast.11), calls=%async_computation.3 | async-start | bytes 393216 | tf_op jit(solution)/shard_map/all_to_all | solution.py:58
  24.7 0.7 copy-start
  25.4 11.2 %all-to-all-start.2 = ((bf16[8,48,256]{2,1,0:T(8,128)(2,1)}), bf16[8,48,256]{2,1,0:T(8,128)(2,1)S(1)}, u32[]{:S(2)}, u32[]{:S(2)}) async-start(bf16[8,48,256]{2,1,0:T(8,128)(2,1)} %bitcast.9), calls=%async_computation.2 | async-start | bytes 393216 | tf_op jit(solution)/shard_map/all_to_all | solution.py:59
  36.5 4.3 %copy-start.2 = (bf16[128,1792]{1,0:T(8,128)(2,1)S(1)}, bf16[128,1792]{1,0:T(8,128)(2,1)}, u32[]{:S(2)}) copy-start(bf16[128,1792]{1,0:T(8,128)(2,1)} %param.7) | copy-start | bytes 1376260
  36.5 28.3 %all-to-all-start.1 = ((bf16[8,48,1792]{2,1,0:T(8,128)(2,1)}), bf16[8,48,1792]{2,1,0:T(8,128)(2,1)S(1)}, u32[]{:S(2)}, u32[]{:S(2)}) async-start(bf16[8,48,1792]{2,1,0:T(8,128)(2,1)} %bitcast.6), calls=%async_computation.1 | async-start | bytes 2752512 | tf_op jit(solution)/shard_map/all_to_all | solution.py:57
  64.8 40.0 %all-to-all-start = ((bf16[8,48,1792]{2,1,0:T(8,128)(2,1)}), bf16[8,48,1792]{2,1,0:T(8,128)(2,1)}, u32[]{:S(2)}, u32[]{:S(2)}) async-start(bf16[8,48,1792]{2,1,0:T(8,128)(2,1)} %bitcast.4), calls=%async_computation | async-start | bytes 2752512 | tf_op jit(solution)/shard_map/all_to_all | solution.py:56
  69.1 57.8 %all-reduce.2.cloned.1.call-start = ((), (), s32[]{:S(2)}) async-start(), calls=%async_computation.4 | async-start | bytes 1572864 | tf_op jit(solution)/shard_map/psum | solution.py:69
  126.9 5.8 %copy-start.4 = (bf16[384,1024]{1,0:T(8,128)(2,1)S(1)}, bf16[384,1024]{1,0:T(8,128)(2,1)}, u32[]{:S(2)}) copy-start(bf16[384,1024]{1,0:T(8,128)(2,1)} %all-reduce.2.cloned.1.call-done) | copy-start | bytes 2359300
Sparse Core Ops, SparseCore 0:
  73.8 52.9 all-reduce.1
where the time goes:
time: 146 us; the launch traced here: 145 us
  blocking collectives  47.1 us (32%)
  waiting for transfers between devices  25.2 us (17%)
  matrix products  19.7 us (13%)
  starting transfers between devices  17.2 us (12%)
  local copies, waits for them, and re-layouts  16.9 us (12%)
  between operations  14.1 us (10%)
  other arithmetic  4.7 us (3%)
    all_gather x1, blocking collectives, on_device(): lax.all_gather(up_rows, 'gy', axis=1, tiled=True)  27 us
    psum x1, waiting for transfers between devices, on_device(): lax.psum(partial_value.astype(jnp.bfloat16), 'gy').astype(jnp.float32)  22.1 us
    all_gather x1, blocking collectives, on_device(): lax.all_gather(gate_rows, 'gy', axis=1, tiled=True)  20 us
    dot_general x3, matrix products, contract_rows(): lax.dot_general(left, right, (((0,), (0,)), ((), ())), preferred_element_...  15.2 us
    scatter x3, local copies, waits for them, and re-layouts, pack_rows(): jnp.zeros((experts * MOST, values.shape[-1]), values.dtype).at[target]  7.38 us
    all_to_all x1, starting transfers between devices, on_device(): lax.all_to_all(gate_routes, 'gx', split_axis=0, concat_axis=0, tiled=True)  5.2 us
    dot_general x1, matrix products, on_device(): lax.dot_general(rows_grad, weight, (((1,), (1,)), ((), ())), preferred_el...  4.53 us
    all_to_all x1, starting transfers between devices, on_device(): lax.all_to_all(act_routes, 'gx', split_axis=0, concat_axis=0, tiled=True)  4.27 us
  transfers between devices with their start and end apart: 5, of which 2 were waited for; matrix products, arithmetic and copies ran while one was open for 16% of the time, Pallas kernels for 0%

commit v1 on v0

--- a/solution.py
+++ b/solution.py
@@ -4,6 +4,7 @@
 from jax.sharding import PartitionSpec as P
 
 MOST = 48
+_cut_table = lambda load, along_axis: jnp.sum(jax.lax.all_gather(load, along_axis), axis=0)
 
 
 def local_grads(hidden_grad, gate_rows, up_rows):
@@ -66,7 +67,7 @@
         rows_grad, weight, (((1,), (1,)), ((), ())), preferred_element_type=jnp.float32
     )
     rows_act = merge_rows(rows_act)
-    hidden_grad = lax.psum(partial_value.astype(jnp.bfloat16), "gy").astype(jnp.float32)
+    hidden_grad = _cut_table(partial_value.astype(jnp.bfloat16), "gy").astype(jnp.float32)
     gate_full, up_full = (
         lax.all_gather(gate_rows, "gy", axis=1, tiled=True),
         lax.all_gather(up_rows, "gy", axis=1, tiled=True),

time: 146 us -> 159 us (1.089)
  blocking collectives: 47.1 us -> 85.3 us
  waiting for transfers between devices: 25.2 us -> 6.1 us
  starting transfers between devices: 17.2 us -> 10.4 us
  other arithmetic: 4.7 us -> 7.48 us
  matrix products: 19.7 us -> 18 us
    all_to_all x0 -> x1, blocking collectives: none -> 23.8 us  [on_device(): lax.all_to_all(grad_routes, 'gx', split_axis=0, concat_axis=0, tiled=True)]
    psum x1 -> x0, waiting for transfers between devices: 22.1 us -> none  [on_device(): lax.psum(partial_value.astype(jnp.bfloat16), 'gy').astype(jnp.float32)]
    all_gather x1, blocking collectives: 20 us -> 30.6 us  [on_device(): lax.all_gather(gate_rows, 'gy', axis=1, tiled=True)]
    all_to_all x1 -> x0, starting transfers between devices: 4.25 us -> none  [on_device(): lax.all_to_all(grad_routes, 'gx', split_axis=0, concat_axis=0, tiled=True)]
    all_gather x1, blocking collectives: 27 us -> 30.8 us  [on_device(): lax.all_gather(up_rows, 'gy', axis=1, tiled=True)]
    reduce_sum x0 -> x1, other arithmetic: none -> 3.63 us  [jnp.sum(jax.lax.all_gather(load, along_axis), axis=0)]
    all_to_all x1, waiting for transfers between devices: 0.01 us -> 2.12 us  [on_device(): lax.all_to_all(up_routes, 'gx', split_axis=0, concat_axis=0, tiled=True)]
    all_to_all x1, starting transfers between devices: 5.2 us -> 3.39 us  [on_device(): lax.all_to_all(gate_routes, 'gx', split_axis=0, concat_axis=0, tiled=True)]
  transfers between devices with their start and end apart: 5 -> 4, of which waited for: 2 -> 2; matrix products, arithmetic and copies ran while one was open for 16% -> 10% of each run, Pallas kernels for 0% -> 0%
where the time goes in v1:
time: 159 us
  blocking collectives  85.3 us (54%)
  matrix products  18 us (11%)
  local copies, waits for them, and re-layouts  17.2 us (11%)
  between operations  14.2 us (9%)
  starting transfers between devices  10.4 us (7%)
  other arithmetic  7.48 us (5%)
  waiting for transfers between devices  6.1 us (4%)
    all_gather x1, blocking collectives, on_device(): lax.all_gather(up_rows, 'gy', axis=1, tiled=True)  30.8 us
    all_gather x1, blocking collectives, on_device(): lax.all_gather(gate_rows, 'gy', axis=1, tiled=True)  30.6 us
    all_to_all x1, blocking collectives, on_device(): lax.all_to_all(grad_routes, 'gx', split_axis=0, concat_axis=0, tiled=True)  23.8 us
    dot_general x3, matrix products, contract_rows(): lax.dot_general(left, right, (((0,), (0,)), ((), ())), preferred_element_...  13.4 us
    scatter x3, local copies, waits for them, and re-layouts, pack_rows(): jnp.zeros((experts * MOST, values.shape[-1]), values.dtype).at[target]  7.39 us
    dot_general x1, matrix products, on_device(): lax.dot_general(rows_grad, weight, (((1,), (1,)), ((), ())), preferred_el...  4.57 us
    all_to_all x1, waiting for transfers between devices, on_device(): lax.all_to_all(gate_routes, 'gx', split_axis=0, concat_axis=0, tiled=True)  3.95 us
    reduce_sum x1, other arithmetic, jnp.sum(jax.lax.all_gather(load, along_axis), axis=0)  3.63 us
  transfers between devices with their start and end apart: 4, of which 2 were waited for; matrix products, arithmetic and copies ran while one was open for 10% of the time, Pallas kernels for 0%

profile of v1, /device:TPU:0, one launch (start us, length us, event | category | flops | bytes accessed | tf_op | source)
XLA Modules:
  0.0 158.5 jit_solution(3381916143588063899)
XLA Ops:
  7.2 0.7 broadcast_multiply_fusion
  7.9 0.8 copy.11
  9.2 0.6 reduce-window.6
  10.1 0.8 copy.13
  11.0 2.7 %broadcast_in_dim.21 = f32[128,2,1792]{2,1,0:T(2,128)} broadcast(bf16[128,1792]{1,0:T(8,128)(2,1)} %param.8), dimensions={0,2} | broadcast | bytes 2293760 | tf_op jit(solution)/shard_map/broadcast_in_dim | solution.py:51
  13.7 2.5 %convert_element_type.52 = f32[256,1792]{1,0:T(8,128)S(1)} reshape(f32[128,2,1792]{2,1,0:T(2,128)} %broadcast_in_dim.21) | data formatting | bytes 3670016 | tf_op jit(solution)/shard_map/convert_element_type | solution.py:51
  16.4 2.4 %scatter_custom_fusion.1 = bf16[384,1792]{1,0:T(8,128)(2,1)S(1)} fusion(s32[256]{0:T(256)S(1)} %bitcast.47, f32[256,1792]{1,0:T(8,128)S(1)} %convert_element_type.52, f32[256]{0:T(256)S(1)} %mul.54, bf16[]{:T(256)} %constant.5.clone.1), kind=kCustom, calls=%fused_computation.29 | custom fusion | flops 917504 | bytes 3212290 | tf_op jit(solution)/shard_map/scatter | solution.py:37
  18.8 23.8 %all_to_all.20 = bf16[8,48,1792]{2,1,0:T(8,128)(2,1)S(1)} all-to-all(bf16[8,48,1792]{2,1,0:T(8,128)(2,1)S(1)} %bitcast.38), channel_id=1, replica_groups=mesh['gx'=8,'gy'=4] {'gx'}, dimensions={0} | all-to-all | bytes 2752512 | tf_op jit(solution)/shard_map/all_to_all | solution.py:58
  42.7 1.1 copy-done
  43.8 4.6 %fusion.14 = bf16[384,1024]{1,0:T(8,128)(2,1)} fusion(bf16[384,1792]{1,0:T(8,128)(2,1)S(1)} %bitcast.40, bf16[1,1024,1792]{2,1,0:T(8,128)(2,1)} %param.13), kind=kOutput, calls=%fused_computation.28 | convolution fusion | flops 1409679360 | bytes 5832704 | tf_op jit(solution)/shard_map/dot_general | solution.py:66
  48.4 2.1 %scatter_custom_fusion.3 = bf16[384,256]{1,0:T(8,128)(2,1)} fusion(s32[256]{0:T(256)S(1)} %bitcast.48, bf16[256,256]{1,0:T(8,128)(2,1)S(1)} %reshape.129, bf16[]{:T(256)} %constant.5.clone.1), kind=kCustom, calls=%fused_computation.35 | custom fusion | bytes 196610 | tf_op jit(solution)/shard_map/scatter | solution.py:37
  50.5 3.4 %all-to-all-start.3 = ((bf16[8,48,256]{2,1,0:T(8,128)(2,1)}), bf16[8,48,256]{2,1,0:T(8,128)(2,1)S(1)}, u32[]{:S(2)}, u32[]{:S(2)}) async-start(bf16[8,48,256]{2,1,0:T(8,128)(2,1)} %bitcast.12), calls=%async_computation.3 | async-start | bytes 393216 | tf_op jit(solution)/shard_map/all_to_all | solution.py:59
  54.0 2.1 %scatter_custom_fusion.2 = bf16[384,256]{1,0:T(8,128)(2,1)} fusion(s32[256]{0:T(256)S(1)} %bitcast.49, bf16[256,256]{1,0:T(8,128)(2,1)S(1)} %reshape.121, bf16[]{:T(256)} %constant.5.clone.1), kind=kCustom, calls=%fused_computation.37 | custom fusion | bytes 196610 | tf_op jit(solution)/shard_map/scatter | solution.py:37
  56.1 4.0 %all-to-all-done.3 = bf16[8,48,256]{2,1,0:T(8,128)(2,1)S(1)} async-done(((bf16[8,48,256]{2,1,0:T(8,128)(2,1)}), bf16[8,48,256]{2,1,0:T(8,128)(2,1)S(1)}, u32[]{:S(2)}, u32[]{:S(2)}) %all-to-all-start.3) | async-done | bytes 196640 | tf_op jit(solution)/shard_map/all_to_all | solution.py:59
  60.1 3.4 %all-to-all-start.2 = ((bf16[8,48,256]{2,1,0:T(8,128)(2,1)}), bf16[8,48,256]{2,1,0:T(8,128)(2,1)S(1)}, u32[]{:S(2)}, u32[]{:S(2)}) async-start(bf16[8,48,256]{2,1,0:T(8,128)(2,1)} %bitcast.10), calls=%async_computation.2 | async-start | bytes 393216 | tf_op jit(solution)/shard_map/all_to_all | solution.py:60
  64.3 3.2 %scatter_custom_fusion = bf16[384,1792]{1,0:T(8,128)(2,1)} fusion(s32[256]{0:T(256)S(1)} %bitcast.50, bf16[256,1792]{1,0:T(8,128)(2,1)S(1)} %reshape.105, bf16[]{:T(256)} %constant.5.clone.1), kind=kCustom, calls=%fused_computation.33 | custom fusion | bytes 1376258 | tf_op jit(solution)/shard_map/scatter | solution.py:37
  67.5 2.1 %all-to-all-done.2 = bf16[8,48,256]{2,1,0:T(8,128)(2,1)S(1)} async-done(((bf16[8,48,256]{2,1,0:T(8,128)(2,1)}), bf16[8,48,256]{2,1,0:T(8,128)(2,1)S(1)}, u32[]{:S(2)}, u32[]{:S(2)}) %all-to-all-start.2) | async-done | bytes 196640 | tf_op jit(solution)/shard_map/all_to_all | solution.py:60
  69.6 3.6 %all-to-all-start = ((bf16[8,48,1792]{2,1,0:T(8,128)(2,1)}), bf16[8,48,1792]{2,1,0:T(8,128)(2,1)S(1)}, u32[]{:S(2)}, u32[]{:S(2)}) async-start(bf16[8,48,1792]{2,1,0:T(8,128)(2,1)} %bitcast.4), calls=%async_computation | async-start | bytes 2752512 | tf_op jit(solution)/shard_map/all_to_all | solution.py:57
  73.2 30.6 %all_gather.15 = bf16[384,1024]{1,0:T(8,128)(2,1)S(1)} all-gather(bf16[384,256]{1,0:T(8,128)(2,1)S(1)} %bitcast.44), channel_id=1, replica_groups=mesh['gx'=8,'gy'=4] {'gy'}, dimensions={1}, use_global_device_ids=true | all-gather | bytes 983040 | tf_op jit(solution)/shard_map/all_gather | solution.py:72
  103.8 30.8 %all_gather.14 = bf16[384,1024]{1,0:T(8,128)(2,1)S(1)} all-gather(bf16[384,256]{1,0:T(8,128)(2,1)S(1)} %bitcast.45), channel_id=1, replica_groups=mesh['gx'=8,'gy'=4] {'gy'}, dimensions={1}, use_global_device_ids=true | all-gather | bytes 983040 | tf_op jit(solution)/shard_map/all_gather | solution.py:73
  134.6 4.0 %fusion.4 = bf16[1,1024,1792]{2,1,0:T(8,128)(2,1)} fusion(bf16[384,1792]{1,0:T(8,128)(2,1)S(1)} %bitcast.41, bf16[384,1024]{1,0:T(8,128)(2,1)S(1)} %all_gather.14, bf16[384,1024]{1,0:T(8,128)(2,1)S(1)} %all_gather.15), kind=kOutput, calls=%fused_computation.11 | convolution fusion | flops 1414266880 | bytes 6619136 | tf_op jit(solution)/shard_map/dot_general | solution.py:24
  138.7 3.6 %reduce_sum.25 = bf16[384,1024]{1,0:T(8,128)(2,1)} reduce(bf16[4,384,1024]{2,1,0:T(8,128)(2,1)} %bitcast.39, bf16[]{:T(256)} %constant.5.clone.1), dimensions={0}, to_apply=%region_5.6 | reduce | flops 1179648 | bytes 3932162 | tf_op jit(solution)/shard_map/reduce_sum | solution.py:7
  142.3 5.3 %fusion.2 = bf16[1,1792,1024]{2,1,0:T(8,128)(2,1)} fusion(bf16[384,1792]{1,0:T(8,128)(2,1)S(1)} %bitcast.42, bf16[384,1024]{1,0:T(8,128)(2,1)S(1)} %all_gather.14, bf16[384,1024]{1,0:T(8,128)(2,1)} %reduce_sum.25, bf16[384,1024]{1,0:T(8,128)(2,1)S(1)} %all_gather.15), kind=kOutput, calls=%fused_computation.9 | convolution fusion | flops 1416232960 | bytes 7405568 | tf_op jit(solution)/shard_map/dot_general | solution.py:24
  147.6 4.1 %fusion.3 = bf16[1,1792,1024]{2,1,0:T(8,128)(2,1)} fusion(bf16[384,1792]{1,0:T(8,128)(2,1)S(1)} %bitcast.43, bf16[384,1024]{1,0:T(8,128)(2,1)S(1)} %copy-done.2, bf16[384,1024]{1,0:T(8,128)(2,1)S(1)} %all_gather.15), kind=kOutput, calls=%fused_computation.10 | convolution fusion | flops 1414266880 | bytes 6619136 | tf_op jit(solution)/shard_map/dot_general | solution.py:24
  (30 shorter events, 2.0 us)
Async XLA Ops:
  7.2 131.5 %all-gather.3.cloned.1.call-start = ((), (), s32[]{:S(2)}) async-start(), calls=%async_computation.4 | async-start | bytes 3932160 | tf_op jit(solution)/shard_map/all_gather | solution.py:7
  42.7 1.1 copy-start
  43.8 4.6 %copy-start.4 = (bf16[128,2,256]{2,1,0:T(2,128)(2,1)S(1)}, bf16[128,2,256]{2,1,0:T(2,128)(2,1)}, u32[]{:S(2)}) copy-start(bf16[128,2,256]{2,1,0:T(2,128)(2,1)} %param.9) | copy-start | bytes 393220
  48.3 5.6 %copy-start.5 = (bf16[128,2,256]{2,1,0:T(2,128)(2,1)S(1)}, bf16[128,2,256]{2,1,0:T(2,128)(2,1)}, u32[]{:S(2)}) copy-start(bf16[128,2,256]{2,1,0:T(2,128)(2,1)} %param.10) | copy-start | bytes 393220
  48.3 15.1 %copy-start.3 = (bf16[128,1792]{1,0:T(8,128)(2,1)S(1)}, bf16[128,1792]{1,0:T(8,128)(2,1)}, u32[]{:S(2)}) copy-start(bf16[128,1792]{1,0:T(8,128)(2,1)} %param.7) | copy-start | bytes 1376260
  50.5 9.5 %all-to-all-start.3 = ((bf16[8,48,256]{2,1,0:T(8,128)(2,1)}), bf16[8,48,256]{2,1,0:T(8,128)(2,1)S(1)}, u32[]{:S(2)}, u32[]{:S(2)}) async-start(bf16[8,48,256]{2,1,0:T(8,128)(2,1)} %bitcast.12), calls=%async_computation.3 | async-start | bytes 393216 | tf_op jit(solution)/shard_map/all_to_all | solution.py:59
  60.1 9.5 %all-to-all-start.2 = ((bf16[8,48,256]{2,1,0:T(8,128)(2,1)}), bf16[8,48,256]{2,1,0:T(8,128)(2,1)S(1)}, u32[]{:S(2)}, u32[]{:S(2)}) async-start(bf16[8,48,256]{2,1,0:T(8,128)(2,1)} %bitcast.10), calls=%async_computation.2 | async-start | bytes 393216 | tf_op jit(solution)/shard_map/all_to_all | solution.py:60
  69.6 72.7 %all-to-all-start = ((bf16[8,48,1792]{2,1,0:T(8,128)(2,1)}), bf16[8,48,1792]{2,1,0:T(8,128)(2,1)S(1)}, u32[]{:S(2)}, u32[]{:S(2)}) async-start(bf16[8,48,1792]{2,1,0:T(8,128)(2,1)} %bitcast.4), calls=%async_computation | async-start | bytes 2752512 | tf_op jit(solution)/shard_map/all_to_all | solution.py:57
  73.2 61.4 %copy-start.1 = (bf16[8,48,1792]{2,1,0:T(8,128)(2,1)S(1)}, bf16[8,48,1792]{2,1,0:T(8,128)(2,1)}, u32[]{:S(2)}) copy-start(bf16[8,48,1792]{2,1,0:T(8,128)(2,1)} %copy-done) | copy-start | bytes 4128772
  142.3 5.3 %copy-start.2 = (bf16[384,1024]{1,0:T(8,128)(2,1)S(1)}, bf16[384,1024]{1,0:T(8,128)(2,1)}, u32[]{:S(2)}) copy-start(bf16[384,1024]{1,0:T(8,128)(2,1)} %reduce_sum.25) | copy-start | bytes 2359300
Sparse Core Ops, SparseCore 0:
  48.5 87.7 all-gather.2
